TPU v7x, 32 devices: a whole 2x2x4 slice. The times are simulated.
32 devices in a mesh: front: 4 (over y, core), row: 4 (over z), col: 2 (over x).
Axes of the slice: x: 2, y: 2, z: 4, core: 2. Of those that a mesh axis runs over, the one named last changes fastest.
Arguments:
- pivot_block: bfloat16 [4, 1024, 1024], P('front'), may hold values from -6 to 6
- border: bfloat16 [4, 8192, 1024], P('front', 'row'), may hold values from -6 to 6
- contrib: bfloat16 [4, 8192, 8192], P('front', 'row', 'col'), may hold values from -6 to 6
- inverses: bfloat16 [4, 4, 256, 256], P('front'), may hold values from -0.0625 to 0.0625
- row_tiles: int32 [4, 64], replicated, may hold values from 0 to 79, as said below
- col_tiles: int32 [4, 64], replicated, may hold values from 0 to 79, as said below
- owner: int32 [80], replicated, may hold values from 0 to 79, as said below
- schur_init: bfloat16 [10240, 10240], P(('front', 'row'), 'col'), may hold values from -6 to 6
- block: bfloat16 [10240, 512], P('col'), may hold values from -0.0625 to 0.0625
Outputs:
- schur: float32 [10240, 10240], P(('front', 'row'), 'col')
- product: float32 [10240, 512], P(('front', 'row', 'col'))
Inputs may be any that keep to these rules, and one draw needn't show every extreme that they name: owner is a permutation of 0 .. 79. For each front the 64 entries are distinct. With s = owner[row_tiles[f, i]], each front has exactly 4 entries in each group s // 5; among the 16 entries of one aligned block of a front at most 2 fall in one group, and that many in some block of every draw. For each front the 64 entries are distinct. With s = owner[col_tiles[f, j]], each front has exactly 32 entries in each group s // 40; among the 32 entries of one aligned block of a front at most 32 fall in one group, and that many in some block of every draw.
All inputs are finite; a program needn't handle non-finite values.
Results may differ from a plain program's by a relative error of at most 0.008.
Values may be sent and summed in bfloat16 or wider, within the bound.
No kernel may reach another device: no remote copies, remote signals or barrier semaphores. Data moves between devices by JAX's collectives and lax.ppermute only.
A program may use at most 256 MiB of HBM per device.

v0:
```python
import jax
import jax.numpy as jnp
from jax import lax
from jax.sharding import PartitionSpec as P

TILE = 128


def eliminate(pivot, rows, inverse_set):
    panels = inverse_set.shape[0]
    width = inverse_set.shape[1]
    pivot_now = pivot.astype(jnp.float32)
    rows_now = rows.astype(jnp.float32)
    leaves = []
    for panel_index in range(panels):
        start = panel_index * width
        left = pivot_now[:, start : start + width].astype(jnp.bfloat16)
        below = jnp.arange(pivot.shape[0])[:, None] >= start + width
        lower = jnp.where(
            below, jnp.dot(left, inverse_set[panel_index], preferred_element_type=jnp.float32), 0.0
        ).astype(jnp.bfloat16)
        side = jnp.dot(
            rows_now[:, start : start + width].astype(jnp.bfloat16),
            inverse_set[panel_index],
            preferred_element_type=jnp.float32,
        ).astype(jnp.bfloat16)
        pivot_now = pivot_now - lax.dot_general(
            lower, lower, (((1,), (1,)), ((), ())), preferred_element_type=jnp.float32
        )
        rows_now = rows_now - lax.dot_general(
            side, lower, (((1,), (1,)), ((), ())), preferred_element_type=jnp.float32
        )
        leaves.append(side)
    return jnp.concatenate(leaves, axis=1)


def route_tables(slots, per_group):
    group = slots // per_group
    within = slots % per_group
    count = slots.shape[-1]
    same = group[..., :, None] == group[..., None, :]
    earlier = jnp.arange(count)[None, :] < jnp.arange(count)[:, None]
    rank = jnp.sum((same & earlier).astype(jnp.int32), axis=-1)
    return (group, rank, within)


def pick_sources(group, rank, n_groups, capacity):
    count = group.shape[-1]
    match = (group[None, None, :] == jnp.arange(n_groups)[:, None, None]) & (
        rank[None, None, :] == jnp.arange(capacity)[None, :, None]
    )
    return jnp.sum(match.astype(jnp.int32) * jnp.arange(count)[None, None, :], axis=-1)


def shards(pivot_block, border, contrib, inverses, row_tiles, col_tiles, owner, schur_init, block):
    n_front = lax.axis_size("front")
    n_row = lax.axis_size("row")
    n_col = lax.axis_size("col")
    front_index = lax.axis_index("front")
    row_index = lax.axis_index("row")
    col_index = lax.axis_index("col")
    groups = n_front * n_row
    tiles_all = row_tiles.shape[1]
    slots_all = owner.shape[0]
    row_span = border.shape[1]
    col_span = contrib.shape[2]
    tile_rows = row_span // TILE
    tile_cols = col_span // TILE
    rows_per_group = slots_all // groups
    cols_per_group = slots_all // n_col
    cap_rows = 2 * tiles_all // (n_row * groups)
    cap_cols = 2 * tiles_all // (n_col * n_col)
    share = row_span // n_col
    own_rows = lax.dynamic_slice_in_dim(border[0], col_index * share, share, 0)
    leaves = eliminate(pivot_block[0], own_rows, inverses[0])
    factor = lax.all_gather(leaves, ("row", "col"), axis=0, tiled=True)
    mine = lax.dynamic_slice_in_dim(factor, row_index * row_span, row_span, 0)
    theirs = lax.dynamic_slice_in_dim(factor, col_index * col_span, col_span, 0)
    update = (
        contrib[0].astype(jnp.float32)
        - lax.dot_general(
            mine, theirs, (((1,), (1,)), ((), ())), preferred_element_type=jnp.float32
        )
    ).astype(jnp.bfloat16)
    tiles = update.reshape(tile_rows, TILE, tile_cols, TILE)
    slot_rows = owner[row_tiles].reshape(n_front, n_row, tile_rows)
    slot_cols = owner[col_tiles].reshape(n_front, n_col, tile_cols)
    group_rows, rank_rows, within_rows = route_tables(slot_rows, rows_per_group)
    group_cols, rank_cols, within_cols = route_tables(slot_cols, cols_per_group)
    send_rows = pick_sources(
        group_rows[front_index, row_index], rank_rows[front_index, row_index], groups, cap_rows
    )
    my_group = front_index * n_row + row_index
    flat_group = group_rows.reshape(groups, tile_rows)
    flat_rank = rank_rows.reshape(groups, tile_rows)
    flat_within = within_rows.reshape(groups, tile_rows)
    hit_rows = (flat_group == my_group)[:, None, :] & (
        flat_rank[:, None, :] == jnp.arange(cap_rows)[None, :, None]
    )
    place_rows = jnp.sum(
        (
            hit_rows[None]
            & (flat_within[None, :, None, :] == jnp.arange(rows_per_group)[:, None, None, None])
        ).astype(jnp.int32),
        axis=-1,
    ).astype(jnp.bfloat16)
    hit_cols = (group_cols == col_index)[:, :, None, :] & (
        rank_cols[:, :, None, :] == jnp.arange(cap_cols)[None, None, :, None]
    )
    place_cols = jnp.sum(
        (
            hit_cols[None]
            & (
                within_cols[None, :, :, None, :]
                == jnp.arange(cols_per_group)[:, None, None, None, None]
            )
        ).astype(jnp.int32),
        axis=-1,
    ).astype(jnp.bfloat16)
    place_cols = jnp.repeat(place_cols, n_row, axis=1)
    send_cols = pick_sources(
        group_cols[front_index, col_index], rank_cols[front_index, col_index], n_col, cap_cols
    )
    by_rows = jnp.take(tiles, send_rows.reshape(-1), axis=0)
    by_both = jnp.take(by_rows, send_cols.reshape(-1), axis=2)
    outgoing = by_both.reshape(groups, cap_rows, TILE, n_col, cap_cols, TILE).transpose(
        0, 3, 1, 4, 2, 5
    )
    outgoing = outgoing.reshape(groups * n_col, cap_rows, cap_cols, TILE, TILE)
    received = lax.all_to_all(
        outgoing, ("front", "row", "col"), split_axis=0, concat_axis=0, tiled=True
    )
    received = received.reshape(groups, n_col, cap_rows, cap_cols, TILE, TILE)
    gathered = jnp.einsum(
        "bgcm,gckmxy->bgkxy", place_cols, received, preferred_element_type=jnp.float32
    ).astype(jnp.bfloat16)
    summed = jnp.einsum("agk,bgkxy->abxy", place_rows, gathered, preferred_element_type=jnp.float32)
    schur = schur_init.astype(jnp.float32) + summed.transpose(0, 2, 1, 3).reshape(
        rows_per_group * TILE, cols_per_group * TILE
    )
    rounded = schur.astype(jnp.bfloat16)
    product = lax.psum_scatter(
        jnp.dot(rounded, block, preferred_element_type=jnp.float32),
        "col",
        scatter_dimension=0,
        tiled=True,
    )
    return (schur, product)


def solution(mesh):
    in_specs = (
        P("front", None, None),
        P("front", "row", None),
        P("front", "row", "col"),
        P("front", None, None, None),
        P(),
        P(),
        P(),
        P(("front", "row"), "col"),
        P("col", None),
    )
    out_specs = (P(("front", "row"), "col"), P(("front", "row", "col"), None))
    return jax.shard_map(shards, mesh=mesh, in_specs=in_specs, out_specs=out_specs, check_vma=False)
```

profile of v0, /device:TPU:0, one launch (start us, length us, event | category | flops | bytes accessed | tf_op | source)
XLA Modules:
  0.0 2108.5 jit_solution(10007459200147742277)
XLA Ops:
  7.3 1.9 dynamic-slice_bitcast_fusion
  9.2 1.2 convolution_convert_fusion.3
  10.8 0.7 convert_subtract_fusion.1
  11.6 0.8 convert_subtract_fusion.2
  13.5 2.8 fusion.59
  16.3 0.8 convolution_subtract_fusion
  17.1 2.0 copy-done.4
  19.4 4.5 fusion.21
  23.9 1.9 convolution_convert_fusion
  25.9 1.5 pad_maximum_fusion
  27.5 2.2 gather_fusion
  32.6 1.9 gather_fusion.1
  34.7 0.6 broadcast_compare_fusion.1
  35.7 0.6 copy-done.11
  36.6 221.0 %all-gather.2.cloned.1.call-done = bf16[8192,1024]{0,1:T(8,128)(2,1)} async-done(((bf16[1024,1024]{0,1:T(8,128)(2,1)}), bf16[8192,1024]{0,1:T(8,128)(2,1)}) %all-gather.2.cloned.1.call-update) | async-done | bytes 16777232 | tf_op jit(solution)/shard_map/all_gather | solution.py:76
  257.6 25.7 %fusion.12 = bf16[256,8,32,128]{3,1,2,0:T(8,128)(2,1)} fusion(bf16[8192,1024]{0,1:T(8,128)(2,1)} %all-gather.2.cloned.1.call-done, s32[]{:T(128)S(6)} %select_n.154, bf16[1,2048,4096]{2,1,0:T(8,128)(2,1)} %param.11, s32[]{:T(128)S(6)} %select_n.153), kind=kOutput, calls=%fused_computation.17 | convolution fusion | flops 17205035008 | bytes 46137352 | tf_op jit(solution)/shard_map/dot_general | solution.py:81
  283.3 15.1 copy.36
  298.3 18.7 gather_fusion.2
  317.1 22.8 %broadcast_select_fusion = bf16[32,128,32,128]{3,2,1,0:T(8,128)(2,1)} fusion(bf16[32,128,32,128]{3,2,1,0:T(8,128)(2,1)} %gather_fusion.2, pred[32]{0:T(512)(128)(4,1)S(1)} %compare_and_fusion.1), kind=kLoop, calls=%fused_computation.13 | loop fusion | flops 16777216 | bytes 67108896 | tf_op jit(solution)/shard_map/jit(_take)/select_n | solution.py:124
  339.9 23.4 %copy.24 = bf16[32,128,32,128]{3,1,0,2:T(8,128)(2,1)} copy(bf16[32,128,32,128]{3,2,1,0:T(8,128)(2,1)} %broadcast_select_fusion) | data formatting | bytes 67108864 | tf_op jit(solution)/shard_map/jit(_take)/select_n | solution.py:124
  363.3 35.9 %gather_fusion.3 = bf16[64,32,128,128]{3,2,1,0:T(8,128)(2,1)} fusion(bf16[32,128,32,128]{3,1,0,2:T(8,128)(2,1)} %copy.24, s32[1024]{0:T(1024)S(1)} %pad_clamp_fusion), kind=kCustom, calls=%fused_computation.3 | custom fusion | bytes 134217984 | tf_op jit(solution)/shard_map/jit(_take)/gather | solution.py:125
  399.2 44.4 %copy_select_fusion = bf16[16,2,128,2,32,128]{5,2,4,1,3,0:T(8,128)(2,1)} fusion(bf16[16,2,128,2,32,128]{5,2,1,0,4,3:T(8,128)(2,1)} %bitcast.16, pred[2,32]{1,0:T(4,128)(4,1)S(1)} %compare_and_fusion.2), kind=kLoop, calls=%fused_computation.7 | loop fusion | flops 33554432 | bytes 134217792 | tf_op jit(solution)/shard_map/jit(_take)/select_n | solution.py:125
  443.7 5.1 all-to-all-start
  449.1 2.0 convert_reduce_fusion
  451.6 1442.9 %all-to-all-done = bf16[32,2,32,128,128]{4,3,2,1,0:T(8,128)(2,1)} async-done(((bf16[32,2,32,128,128]{4,3,2,1,0:T(8,128)(2,1)}), bf16[32,2,32,128,128]{4,3,2,1,0:T(8,128)(2,1)}, u32[]{:S(2)}, u32[]{:S(2)}) %all-to-all-start) | async-done | bytes 67108896 | tf_op jit(solution)/shard_map/all_to_all | solution.py:130
  1894.6 66.8 %fusion.2 = bf16[40,16,2,128,128]{4,0,3,2,1:T(8,128)(2,1)} fusion(bf16[40,16,2,32,1,1]{0,3,2,5,4,1:T(8,128)(2,1)S(1)} %bitcast.89, bf16[16,2,2,32,128,128]{5,4,3,2,1,0:T(8,128)(2,1)} %bitcast.19), kind=kOutput, calls=%fused_computation.8 | convolution fusion | flops 2705326080 | bytes 109133824 | tf_op jit(solution)/shard_map/bgcm,gckmxy->bgkxy/dot_general | solution.py:134
  1961.4 34.2 %fusion.8 = f32[5,128,40,128]{3,0,1,2:T(8,128)} fusion(bf16[40,16,2,128,128]{4,0,3,2,1:T(8,128)(2,1)} %fusion.2, bf16[5,16,2,1,1]{1,2,0,4,3:T(2,128)(2,1)S(1)} %convert_bitcast_fusion), kind=kOutput, calls=%fused_computation.15 | convolution fusion | flops 209715200 | bytes 55050560 | tf_op jit(solution)/shard_map/agk,bgkxy->abxy/dot_general | solution.py:137
  1995.6 9.8 copy.29
  2005.4 6.0 bitcast_add_fusion
  2011.4 4.9 copy-done.2
  2016.4 4.6 fusion.15
  2021.0 80.4 %reduce-scatter.2.cloned.1.call-done = f32[320,512]{1,0:T(8,128)} async-done(((f32[640,512]{1,0:T(8,128)}), f32[320,512]{1,0:T(8,128)}) %reduce-scatter.2.cloned.1.call-update) | async-done | bytes 655376 | tf_op jit(solution)/shard_map/reduce_scatter | solution.py:142
  (106 shorter events, 6.5 us)
Async XLA Ops:
  7.2 20.4 copy-start
  7.2 3.3 copy-start.6
  7.2 3.3 copy-start.5
  7.2 250.4 %all-gather.2.cloned.1.call-start = ((), (), s32[]{:S(2)}) async-start(), calls=%async_computation.2 | async-start | bytes 18874368 | tf_op jit(solution)/shard_map/all_gather | solution.py:76
  11.6 2.0 copy-start.3
  17.1 2.0 copy-start.4
  23.9 3.5 copy-start.18
  23.9 3.5 copy-start.19
  30.3 253.0 %copy-start.13 = (s32[256]{0:T(256)}, s32[256]{0:T(256)S(1)}, u32[]{:S(2)}) copy-start(s32[256]{0:T(256)S(1)} %get-tuple-element.7) | copy-start | bytes 3076
  31.5 0.6 copy-start.9
  34.5 248.7 %copy-start.7 = (s32[4,2,32]{2,1,0:T(2,128)}, s32[4,2,32]{2,1,0:T(2,128)S(1)}, u32[]{:S(2)}) copy-start(s32[4,2,32]{2,1,0:T(2,128)S(1)} %rem.73) | copy-start | bytes 3076
  35.7 0.6 copy-start.11
  443.6 5.2 copy-start.14
  443.6 5.3 copy-start.8
  443.6 5.4 copy-start.12
  443.6 5.4 copy-start.15
  443.6 7.5 copy-start.16
  443.6 7.6 copy-start.17
  443.6 7.7 copy-start.10
  443.7 1450.9 %all-to-all-start = ((bf16[32,2,32,128,128]{4,3,2,1,0:T(8,128)(2,1)}), bf16[32,2,32,128,128]{4,3,2,1,0:T(8,128)(2,1)}, u32[]{:S(2)}, u32[]{:S(2)}) async-start(bf16[32,2,32,128,128]{4,3,2,1,0:T(8,128)(2,1)} %bitcast.18), calls=%async_computation | async-start | bytes 134217728 | tf_op jit(solution)/shard_map/all_to_all | solution.py:130
  448.8 1652.7 %reduce-scatter.2.cloned.1.call-start = ((), (), s32[]{:S(2)}) async-start(), calls=%async_computation.3 | async-start | bytes 1966080 | tf_op jit(solution)/shard_map/reduce_scatter | solution.py:142
  1961.4 55.0 %slice-start = ((s8[5242880]{0:T(1024)(128)(4,1)}), s8[1048576]{0:T(1024)(128)(4,1)S(1)}, s32[]{:S(2)}) async-start(s8[5242880]{0:T(1024)(128)(4,1)} %bitcast.91), calls=%async_computation.4 | async-start | bytes 2097152
  1995.6 20.7 slice-start.1
  2011.4 5.0 copy-start.2
  2016.4 85.1 %copy-start.1 = (s32[80]{0:T(128)S(1)}, s32[80]{0:T(128)}, u32[]{:S(2)}) copy-start(s32[80]{0:T(128)} %param.15) | copy-start | bytes 964
Sparse Core Ops, SparseCore 0:
  27.5 230.0 all-gather.1
  2021.1 80.2 reduce-scatter.1
where the time goes:
time: 2110 us
  waiting for transfers between devices  1740 us (82%)
  matrix products  145 us (7%)
  local copies, waits for them, and re-layouts  119 us (6%)
  other arithmetic  80 us (4%)
    all_to_all x1, waiting for transfers between devices, shards(): lax.all_to_all(outgoing, ('front', 'row', 'col'), split_axis=0, concat_ax...  1440 us
    all_gather x1, waiting for transfers between devices, shards(): factor = lax.all_gather(leaves, ('row', 'col'), axis=0, tiled=True)  221 us
    reduce_scatter x1, waiting for transfers between devices, shards(): lax.psum_scatter(jnp.dot(rounded, block, preferred_element_type=jnp.float...  80.4 us
    dot_general x1, matrix products, shards(): jnp.einsum('bgcm,gckmxy->bgkxy', place_cols, received, preferred_element_...  66.8 us
    select_n x2, other arithmetic, shards(): by_both = jnp.take(by_rows, send_cols.reshape(-1), axis=2)  44.4 us
  transfers between devices with their start and end apart: 3, of which 3 were waited for; matrix products, arithmetic and copies ran while one was open for 0% of the time, Pallas kernels for 0%

commit v1 on v0

--- a/solution.py
+++ b/solution.py
@@ -1,9 +1,39 @@
+import functools
 import jax
 import jax.numpy as jnp
 from jax import lax
 from jax.sharding import PartitionSpec as P
 
 TILE = 128
+
+
+def treat_the_points(sample, ndim_at):
+    arr_now = list(sample.shape[1:])
+    arr_now[ndim_at] *= sample.shape[0]
+    local_now = jnp.moveaxis(sample, 0, ndim_at).reshape(arr_now)
+    return local_now
+
+
+def number_ends(tile_in, peer_axis):
+    n_all = lax.axis_size(peer_axis)
+    carry = tile_in[None]
+    for hop_no in range(n_all.bit_length() - 1):
+        newest = 1 << hop_no
+        then = lax.ppermute(carry, peer_axis, [(kk, kk ^ newest) for kk in range(n_all)])
+        small = jnp.stack([carry, then], axis=0)
+        side_arr = lax.axis_index(peer_axis)
+        answer = side_arr >> hop_no & 1
+        carry = jnp.where(answer == 0, small, small[::-1]).reshape(-1, *tile_in.shape)
+    return carry
+
+
+def rows_point(q_in, x0, row_dim):
+    tile_out = number_ends(q_in, x0)
+    next_value = treat_the_points(tile_out, row_dim)
+    return next_value
+
+
+follow_patches_on_mesh = functools.partial(rows_point, x0=("row", "col"), row_dim=0)
 
 
 def eliminate(pivot, rows, inverse_set):
@@ -73,7 +103,7 @@
     share = row_span // n_col
     own_rows = lax.dynamic_slice_in_dim(border[0], col_index * share, share, 0)
     leaves = eliminate(pivot_block[0], own_rows, inverses[0])
-    factor = lax.all_gather(leaves, ("row", "col"), axis=0, tiled=True)
+    factor = follow_patches_on_mesh(leaves)
     mine = lax.dynamic_slice_in_dim(factor, row_index * row_span, row_span, 0)
     theirs = lax.dynamic_slice_in_dim(factor, col_index * col_span, col_span, 0)
     update = (

time: 2110 us -> 2450 us (1.16)
  waiting for transfers between devices: 1740 us -> 2000 us
  other arithmetic: 80 us -> 131 us
    ppermute x0 -> x3, waiting for transfers between devices: none -> 475 us  [number_ends(): lax.ppermute(carry, peer_axis, [(kk, kk ^ newest) for kk in range(n_all)])]
    all_gather x1 -> x0, waiting for transfers between devices: 221 us -> none  [shards(): factor = lax.all_gather(leaves, ('row', 'col'), axis=0, tiled=True)]
    another operation x0 -> x5, other arithmetic: none -> 27.9 us  [number_ends(): small = jnp.stack([carry, then], axis=0)]
  transfers between devices with their start and end apart: 3 -> 5, of which waited for: 3 -> 5; matrix products, arithmetic and copies ran while one was open for 0% -> 1% of each run, Pallas kernels for 0% -> 0%
where the time goes in v1:
time: 2450 us; the launch traced here: 2440 us
  waiting for transfers between devices  2000 us (82%)
  matrix products  147 us (6%)
  local copies, waits for them, and re-layouts  141 us (6%)
  other arithmetic  131 us (5%)
    all_to_all x1, waiting for transfers between devices, shards(): lax.all_to_all(outgoing, ('front', 'row', 'col'), split_axis=0, concat_ax...  1440 us
    ppermute x3, waiting for transfers between devices, number_ends(): lax.ppermute(carry, peer_axis, [(kk, kk ^ newest) for kk in range(n_all)])  475 us
    reduce_scatter x1, waiting for transfers between devices, shards(): lax.psum_scatter(jnp.dot(rounded, block, preferred_element_type=jnp.float...  80.4 us
    dot_general x1, matrix products, shards(): jnp.einsum('bgcm,gckmxy->bgkxy', place_cols, received, preferred_element_...  66.8 us
  transfers between devices with their start and end apart: 5, of which 5 were waited for; matrix products, arithmetic and copies ran while one was open for 1% of the time, Pallas kernels for 0%

profile of v1, /device:TPU:0, one launch (start us, length us, event | category | flops | bytes accessed | tf_op | source)
XLA Modules:
  0.0 2444.3 jit_solution(13789329169824528850)
XLA Ops:
  14.0 2.8 fusion.63
  19.9 4.7 fusion.23
  26.6 5.3 fusion.34
  31.8 3.0 collective-permute-start
  34.8 45.9 %collective-permute-done = bf16[1,1024,1024]{1,2,0:T(8,128)(2,1)} collective-permute-done((bf16[1,1024,1024]{1,2,0:T(8,128)(2,1)}, bf16[1,1024,1024]{1,2,0:T(8,128)(2,1)}, u32[]{:S(2)}, u32[]{:S(2)}) %collective-permute-start) | collective-permute-done | bytes 2097184 | tf_op jit(solution)/shard_map/ppermute | solution.py:22
  80.7 2.0 pad_maximum_fusion.2
  82.7 5.1 fusion.19
  89.6 90.2 %collective-permute-done.1 = bf16[2,1024,1024]{1,2,0:T(8,128)(2,1)} collective-permute-done((bf16[2,1024,1024]{1,2,0:T(8,128)(2,1)}, bf16[2,1024,1024]{1,2,0:T(8,128)(2,1)}, u32[]{:S(2)}, u32[]{:S(2)}) %collective-permute-start.1) | collective-permute-done | bytes 4194336 | tf_op jit(solution)/shard_map/ppermute | solution.py:22
  179.8 7.6 pad_maximum_fusion.1
  187.5 13.5 reverse_select_fusion.1
  200.9 11.4 copy.29
  212.3 2.5 collective-permute-start.2
  224.1 11.4 copy.30
  235.5 338.5 %collective-permute-done.2 = bf16[4,1024,1024]{2,1,0:T(8,128)(2,1)} collective-permute-done((bf16[4,1024,1024]{2,1,0:T(8,128)(2,1)}, bf16[4,1024,1024]{2,1,0:T(8,128)(2,1)}, u32[]{:S(2)}, u32[]{:S(2)}) %collective-permute-start.2) | collective-permute-done | bytes 8388640 | tf_op jit(solution)/shard_map/ppermute | solution.py:22
  574.1 8.0 pad_maximum_fusion
  582.1 10.6 reverse_select_fusion
  592.7 26.4 %fusion.12 = bf16[256,8,32,128]{3,1,2,0:T(8,128)(2,1)} fusion(bf16[8192,1024]{1,0:T(8,128)(2,1)} %bitcast.104, s32[]{:T(128)S(6)} %select_n.184, bf16[1,2048,4096]{2,1,0:T(8,128)(2,1)} %param.11, s32[]{:T(128)S(6)} %select_n.183), kind=kOutput, calls=%fused_computation.21 | convolution fusion | flops 17205035008 | bytes 46137352 | tf_op jit(solution)/shard_map/dot_general | solution.py:111
  619.1 15.1 copy.44
  634.1 18.7 gather_fusion.2
  652.9 22.8 broadcast_select_fusion
  675.7 23.4 copy.32
  699.0 35.9 %gather_fusion.3 = bf16[64,32,128,128]{3,2,1,0:T(8,128)(2,1)} fusion(bf16[32,128,32,128]{3,1,0,2:T(8,128)(2,1)} %copy.32, s32[1024]{0:T(1024)S(1)} %pad_clamp_fusion), kind=kCustom, calls=%fused_computation.3 | custom fusion | bytes 134217984 | tf_op jit(solution)/shard_map/jit(_take)/gather | solution.py:155
  734.9 44.2 %copy_select_fusion = bf16[16,2,128,2,32,128]{5,2,4,1,3,0:T(8,128)(2,1)} fusion(bf16[16,2,128,2,32,128]{5,2,1,0,4,3:T(8,128)(2,1)} %bitcast.26, pred[2,32]{1,0:T(4,128)(4,1)S(1)} %copy-done.22), kind=kLoop, calls=%fused_computation.7 | loop fusion | flops 33554432 | bytes 134217792 | tf_op jit(solution)/shard_map/jit(_take)/select_n | solution.py:155
  779.2 5.1 all-to-all-start
  786.9 1443.2 %all-to-all-done = bf16[32,2,32,128,128]{4,3,2,1,0:T(8,128)(2,1)} async-done(((bf16[32,2,32,128,128]{4,3,2,1,0:T(8,128)(2,1)}), bf16[32,2,32,128,128]{4,3,2,1,0:T(8,128)(2,1)}, u32[]{:S(2)}, u32[]{:S(2)}) %all-to-all-start) | async-done | bytes 67108896 | tf_op jit(solution)/shard_map/all_to_all | solution.py:160
  2230.1 66.8 %fusion.2 = bf16[40,16,2,128,128]{4,0,3,2,1:T(8,128)(2,1)} fusion(bf16[40,16,2,32,1,1]{0,3,2,5,4,1:T(8,128)(2,1)S(1)} %bitcast.106, bf16[16,2,2,32,128,128]{5,4,3,2,1,0:T(8,128)(2,1)} %bitcast.29), kind=kOutput, calls=%fused_computation.8 | convolution fusion | flops 2705326080 | bytes 109133824 | tf_op jit(solution)/shard_map/bgcm,gckmxy->bgkxy/dot_general | solution.py:164
  2297.0 34.3 %fusion.8 = f32[5,128,40,128]{3,0,1,2:T(8,128)} fusion(bf16[40,16,2,128,128]{4,0,3,2,1:T(8,128)(2,1)} %fusion.2, bf16[5,16,2,1,1]{1,2,0,4,3:T(2,128)(2,1)S(1)} %convert_bitcast_fusion), kind=kOutput, calls=%fused_computation.18 | convolution fusion | flops 209715200 | bytes 55050560 | tf_op jit(solution)/shard_map/agk,bgkxy->abxy/dot_general | solution.py:167
  2331.3 9.8 copy.37
  2341.1 6.0 bitcast_add_fusion
  2347.1 4.9 copy-done.2
  2352.1 4.6 fusion.15
  2356.7 80.4 %reduce-scatter.2.cloned.1.call-done = f32[320,512]{1,0:T(8,128)} async-done(((f32[640,512]{1,0:T(8,128)}), f32[320,512]{1,0:T(8,128)}) %reduce-scatter.2.cloned.1.call-update) | async-done | bytes 655376 | tf_op jit(solution)/shard_map/reduce_scatter | solution.py:172
  (123 shorter events, 25.3 us)
Async XLA Ops:
  7.2 207.8 %copy-start = (s32[80]{0:T(128)S(1)}, s32[80]{0:T(128)}, u32[]{:S(2)}) copy-start(s32[80]{0:T(128)} %param.15) | copy-start | bytes 964
  7.2 4.6 copy-start.6
  11.8 1.6 copy-start.7
  12.6 4.2 copy-start.3
  16.8 3.1 copy-start.8
  17.6 2.0 copy-start.4
  19.9 4.7 copy-start.5
  31.8 48.9 %collective-permute-start = (bf16[1,1024,1024]{1,2,0:T(8,128)(2,1)}, bf16[1,1024,1024]{1,2,0:T(8,128)(2,1)}, u32[]{:S(2)}, u32[]{:S(2)}) collective-permute-start(bf16[1,1024,1024]{1,2,0:T(8,128)(2,1)} %get-tuple-element.9), channel_id=1, source_target_pairs={{0,1},{1,0},{2,3},{3,2},{4,5},{5,4},{6,7},{7,6},{8,9},{9,8},{10,11... | collective-permute-start | bytes 6291464 | tf_op jit(solution)/shard_map/ppermute | solution.py:22
  87.8 92.1 %collective-permute-start.1 = (bf16[2,1024,1024]{1,2,0:T(8,128)(2,1)}, bf16[2,1024,1024]{1,2,0:T(8,128)(2,1)}, u32[]{:S(2)}, u32[]{:S(2)}) collective-permute-start(bf16[2,1024,1024]{1,2,0:T(8,128)(2,1)} %get-tuple-element.7), channel_id=1, source_target_pairs={{0,2},{1,3},{2,0},{3,1},{4,6},{5,7},{6,4},{7,5},{8,10},{9,11},{10,... | collective-permute-start | bytes 12582920 | tf_op jit(solution)/shard_map/ppermute | solution.py:22
  200.9 13.9 copy-start.20
  200.9 13.9 copy-start.21
  212.3 361.7 %collective-permute-start.2 = (bf16[4,1024,1024]{2,1,0:T(8,128)(2,1)}, bf16[4,1024,1024]{2,1,0:T(8,128)(2,1)}, u32[]{:S(2)}, u32[]{:S(2)}) collective-permute-start(bf16[4,1024,1024]{2,1,0:T(8,128)(2,1)} %copy.29), channel_id=1, source_target_pairs={{0,4},{1,5},{2,6},{3,7},{4,0},{5,1},{6,2},{7,3},{8,12},{9,13},{10,... | collective-permute-start | bytes 25165832 | tf_op jit(solution)/shard_map/ppermute | solution.py:22
  217.4 18.1 copy-start.15
  218.6 0.6 copy-start.11
  221.6 13.9 copy-start.9
  222.7 0.6 copy-start.13
  699.0 35.9 %copy-start.22 = (pred[2,32]{1,0:T(4,128)(4,1)S(1)}, pred[2,32]{1,0:T(4,128)(4,1)}, u32[]{:S(2)}) copy-start(pred[2,32]{1,0:T(4,128)(4,1)} %compare_and_fusion.2) | copy-start | bytes 196
  779.2 5.2 copy-start.16
  779.2 5.3 copy-start.10
  779.2 5.4 copy-start.14
  779.2 5.4 copy-start.17
  779.2 7.2 copy-start.18
  779.2 7.2 copy-start.19
  779.2 7.3 copy-start.12
  779.2 1450.9 %all-to-all-start = ((bf16[32,2,32,128,128]{4,3,2,1,0:T(8,128)(2,1)}), bf16[32,2,32,128,128]{4,3,2,1,0:T(8,128)(2,1)}, u32[]{:S(2)}, u32[]{:S(2)}) async-start(bf16[32,2,32,128,128]{4,3,2,1,0:T(8,128)(2,1)} %bitcast.28), calls=%async_computation | async-start | bytes 134217728 | tf_op jit(solution)/shard_map/all_to_all | solution.py:160
  784.3 1652.9 %reduce-scatter.2.cloned.1.call-start = ((), (), s32[]{:S(2)}) async-start(), calls=%async_computation.2 | async-start | bytes 1966080 | tf_op jit(solution)/shard_map/reduce_scatter | solution.py:172
  2297.0 55.1 %slice-start = ((s8[5242880]{0:T(1024)(128)(4,1)}), s8[1048576]{0:T(1024)(128)(4,1)S(1)}, s32[]{:S(2)}) async-start(s8[5242880]{0:T(1024)(128)(4,1)} %bitcast.108), calls=%async_computation.3 | async-start | bytes 2097152
  2331.3 20.8 slice-start.1
  2347.1 5.0 copy-start.2
  2352.1 85.1 %copy-start.1 = (s32[80]{0:T(128)S(1)}, s32[80]{0:T(128)}, u32[]{:S(2)}) copy-start(s32[80]{0:T(128)} %param.15) | copy-start | bytes 964
Sparse Core Ops, SparseCore 0:
  2356.9 80.2 reduce-scatter.1
